TPU v7x, 512 devices: a whole 4x8x8 slice. The times are simulated.
512 devices in a mesh: gx: 64 (over y, z), gy: 2 (over core), ma: 4 (over x).
Axes of the slice: x: 4, y: 8, z: 8, core: 2. Of those that a mesh axis runs over, the one named last changes fastest.
Arguments:
- ensemble: float32 [80, 2, 256, 256], P('ma', None, 'gx', 'gy'), may hold values from -6 to 6
- wind_field: float32 [2, 2, 256, 256], P(None, None, 'gx', 'gy'), may hold values from -0.45 to 0.45
- obs_value: float32 [4, 1024], replicated, may hold values from -6 to 6
- obs_var: float32 [4, 1024], replicated, may hold values from 2 to 20
- obs_region: int32 [4, 1024], replicated, may hold values from 0 to 127, as said below
- obs_cell: int32 [4, 1024], replicated, may hold values from 0 to 1023
- block_order: int32 [4], replicated, may hold values from 0 to 3, each once
- localization: float32 [64, 2, 4, 1024], P('gx', 'gy'), may hold values from 0 to 1
Outputs:
- analysis: float32 [80, 2, 256, 256], P('ma', None, 'gx', 'gy')
Inputs may be any that keep to these rules, and one draw needn't show every extreme that they name: `obs_region`: region index = first-dimension region * 2 + second-dimension region.
All inputs are finite; a program needn't handle non-finite values.
Results may differ from a plain program's by a relative error of at most 0.0001.
Values sent between devices are 32-bit elements; how exact they have to be, the bound alone decides.
No kernel may reach another device: no remote copies, remote signals or barrier semaphores. Data moves between devices by JAX's collectives and lax.ppermute only.
A program may use at most 64 MiB of HBM per device.

v0:
```python
import jax
import jax.numpy as jnp
from jax import lax
from jax.sharding import PartitionSpec as P

STEPS = 2
BLOCKS = 4
KAPPA = 0.025


def extended(block, sides, width):
    for axis, dim in sides:
        count = lax.axis_size(axis)
        forward = [(i, i + 1) for i in range(count - 1)]
        forward.append((count - 1, 0))
        backward = [(target, source) for source, target in forward]
        low = lax.ppermute(
            lax.slice_in_dim(block, block.shape[dim] - width, None, axis=dim), axis, forward
        )
        high = lax.ppermute(lax.slice_in_dim(block, 0, width, axis=dim), axis, backward)
        block = jnp.concatenate([low, block, high], axis=dim)
    return block


def advect(tracer, wind_field):
    padded = extended(tracer, (("gx", 2), ("gy", 3)), 1)
    east_wind = wind_field[0][None]
    north_wind = wind_field[1][None]
    middle = padded[:, :, 1:-1, 1:-1]
    west_side = padded[:, :, :-2, 1:-1]
    east_side = padded[:, :, 2:, 1:-1]
    south_side = padded[:, :, 1:-1, :-2]
    north_side = padded[:, :, 1:-1, 2:]
    return (
        middle
        - jnp.maximum(east_wind, 0.0) * (middle - west_side)
        - jnp.minimum(east_wind, 0.0) * (east_side - middle)
        - jnp.maximum(north_wind, 0.0) * (middle - south_side)
        - jnp.minimum(north_wind, 0.0) * (north_side - middle)
        + KAPPA * (east_side + west_side + north_side + south_side - 4.0 * middle)
    )


def mixing_matrix(prior_obs, observed, error_var, taper, ensemble_size):
    denom = ensemble_size - 1.0
    obs_mean = jnp.mean(prior_obs, axis=0)
    anomaly = prior_obs - obs_mean
    variance = jnp.sum(anomaly * anomaly, axis=0) / denom
    total_var = variance + error_var
    innovation = observed - obs_mean
    shrink = 1.0 / (1.0 + jnp.sqrt(error_var / total_var))
    gain_mean = taper * innovation / (denom * total_var)
    gain_spread = taper * shrink / (denom * total_var)
    shift_terms = jnp.dot(anomaly, gain_mean, precision=lax.Precision.HIGHEST)
    weighted = anomaly * gain_spread
    return shift_terms[:, None] - jnp.dot(weighted, anomaly.T, precision=lax.Precision.HIGHEST)


def local(
    ensemble, wind_field, obs_value, obs_var, obs_region, obs_cell, block_order, localization
):
    state = ensemble
    for step_index in range(STEPS):
        state = advect(state, wind_field)
    members_dev, levels, cells_x, cells_y = state.shape
    ensemble_size = members_dev * lax.axis_size("ma")
    own_region = lax.axis_index("gx") * lax.axis_size("gy") + lax.axis_index("gy")
    member_part = lax.axis_index("ma")
    stacked = state.reshape(members_dev, -1)
    for position in range(BLOCKS):
        block_id = block_order[position]
        gathered = lax.all_gather(stacked, "ma", axis=0, tiled=True)
        picked = jnp.take(gathered, obs_cell[block_id], axis=1)
        is_held = obs_region[block_id] == own_region
        prior_obs = lax.psum(jnp.where(is_held[None], picked, 0.0), ("gx", "gy"))
        mixing = mixing_matrix(
            prior_obs,
            obs_value[block_id],
            obs_var[block_id],
            localization[0, 0, block_id],
            ensemble_size,
        )
        center = jnp.mean(gathered, axis=0)
        own_columns = lax.dynamic_slice_in_dim(mixing, member_part * members_dev, members_dev, 1)
        stacked = stacked + jnp.dot(
            own_columns.T, gathered - center, precision=lax.Precision.HIGHEST
        )
    return stacked.reshape(state.shape)


def solution(mesh):
    in_specs = (
        P("ma", None, "gx", "gy"),
        P(None, None, "gx", "gy"),
        P(),
        P(),
        P(),
        P(),
        P(),
        P("gx", "gy", None, None),
    )
    out_specs = P("ma", None, "gx", "gy")
    return jax.shard_map(local, mesh=mesh, in_specs=in_specs, out_specs=out_specs, check_vma=False)
```

profile of v0, /device:TPU:24, one launch (start us, length us, event | category | flops | bytes accessed | tf_op | source)
XLA Modules:
  0.0 904.9 jit_solution(8745651643520247778)
XLA Ops:
  7.6 10.8 %collective-permute-start.1 = (f32[20,2,1,128]{3,2,1,0:T(1,128)S(1)}, f32[20,2,1,128]{3,2,1,0:T(1,128)S(1)}, u32[]{:S(2)}, u32[]{:S(2)}) collective-permute-start(f32[20,2,1,128]{3,2,1,0:T(1,128)S(1)} %get-tuple-element.29), channel_id=1, source_target_pairs={{8,0},{16,8},{24,16},{32,24},{40,32},{48,40},{56,48},{64,56},{72,6... | collective-permute-start | bytes 61448 | tf_op jit(solution)/shard_map/ppermute | solution.py:20
  18.4 2.1 collective-permute-start
  29.7 1.9 collective-permute-start.3
  31.7 2.4 collective-permute-start.2
  35.5 6.0 collective-permute-start.5
  41.6 1.9 collective-permute-start.4
  43.6 5.8 collective-permute-done.4
  49.5 1.9 collective-permute-start.7
  51.5 2.4 collective-permute-start.6
  55.4 12.9 %all-gather = f32[4,20,1024]{2,1,0:T(8,128)S(1)} all-gather(f32[1,20,1024]{2,1,0:T(8,128)S(1)} %reshape.117), channel_id=1, replica_groups=mesh['gx'=64,'gy'=2,'ma'=4] {'ma'}, dimensions={0}, use_global_device_ids=true | all-gather | bytes 409600 | tf_op jit(solution)/shard_map/all_gather | solution.py:72
  68.5 2.8 gather_fusion
  71.3 1.1 bitcast_select_fusion.3
  72.6 190.9 %all-reduce.5.cloned.1.call-done = f32[80,1024]{0,1:T(8,128)} async-done(((f32[80,1024]{0,1:T(8,128)}), f32[80,1024]{0,1:T(8,128)}) %all-reduce.5.cloned.1.call-update) | async-done | bytes 327696 | tf_op jit(solution)/shard_map/psum | solution.py:75
  263.5 1.3 reduce_sum.108
  265.6 1.5 fusion.6
  267.9 13.0 %all-gather.1 = f32[4,20,1024]{2,1,0:T(8,128)S(1)} all-gather(f32[1,20,1024]{2,1,0:T(8,128)S(1)} %bitcast.72), channel_id=1, replica_groups=mesh['gx'=64,'gy'=2,'ma'=4] {'ma'}, dimensions={0}, use_global_device_ids=true | all-gather | bytes 409600 | tf_op jit(solution)/shard_map/all_gather | solution.py:72
  281.1 2.8 gather_fusion.1
  283.9 1.1 bitcast_select_fusion.2
  285.2 188.6 %all-reduce.7.cloned.1.call-done = f32[80,1024]{0,1:T(8,128)} async-done(((f32[80,1024]{0,1:T(8,128)}), f32[80,1024]{0,1:T(8,128)}) %all-reduce.7.cloned.1.call-update) | async-done | bytes 327696 | tf_op jit(solution)/shard_map/psum | solution.py:75
  473.7 1.3 reduce_sum.111
  475.5 1.5 fusion.4
  477.8 13.0 %all-gather.2 = f32[4,20,1024]{2,1,0:T(8,128)S(1)} all-gather(f32[1,20,1024]{2,1,0:T(8,128)S(1)} %bitcast.73), channel_id=1, replica_groups=mesh['gx'=64,'gy'=2,'ma'=4] {'ma'}, dimensions={0}, use_global_device_ids=true | all-gather | bytes 409600 | tf_op jit(solution)/shard_map/all_gather | solution.py:72
  491.1 2.8 gather_fusion.2
  493.9 1.1 bitcast_select_fusion.1
  495.3 188.4 %all-reduce.9.cloned.1.call-done = f32[80,1024]{0,1:T(8,128)} async-done(((f32[80,1024]{0,1:T(8,128)}), f32[80,1024]{0,1:T(8,128)}) %all-reduce.9.cloned.1.call-update) | async-done | bytes 327696 | tf_op jit(solution)/shard_map/psum | solution.py:75
  683.7 1.3 reduce_sum.114
  685.5 1.5 fusion.2
  687.7 13.0 %all-gather.3 = f32[4,20,1024]{2,1,0:T(8,128)S(1)} all-gather(f32[1,20,1024]{2,1,0:T(8,128)S(1)} %bitcast.71), channel_id=1, replica_groups=mesh['gx'=64,'gy'=2,'ma'=4] {'ma'}, dimensions={0}, use_global_device_ids=true | all-gather | bytes 409600 | tf_op jit(solution)/shard_map/all_gather | solution.py:72
  701.0 2.8 gather_fusion.3
  705.0 188.6 %all-reduce.11.cloned.1.call-done = f32[80,1024]{0,1:T(8,128)} async-done(((f32[80,1024]{0,1:T(8,128)}), f32[80,1024]{0,1:T(8,128)}) %all-reduce.11.cloned.1.call-update) | async-done | bytes 327696 | tf_op jit(solution)/shard_map/psum | solution.py:75
  893.6 1.3 reduce_sum.117
  895.4 1.5 fusion
  (106 shorter events, 14.1 us)
Async XLA Ops:
  6.5 256.9 %all-reduce.5.cloned.1.call-start = ((), (), s32[]{:S(2)}) async-start(), calls=%async_computation | async-start | bytes 1048576 | tf_op jit(solution)/shard_map/psum | solution.py:75
  7.5 12.9 %copy-start.11 = (s32[4]{0:T(128)S(1)}, s32[4]{0:T(128)}, u32[]{:S(2)}) copy-start(s32[4]{0:T(128)} %param.16) | copy-start | bytes 52
  7.6 22.0 %collective-permute-start.1 = (f32[20,2,1,128]{3,2,1,0:T(1,128)S(1)}, f32[20,2,1,128]{3,2,1,0:T(1,128)S(1)}, u32[]{:S(2)}, u32[]{:S(2)}) collective-permute-start(f32[20,2,1,128]{3,2,1,0:T(1,128)S(1)} %get-tuple-element.29), channel_id=1, source_target_pairs={{8,0},{16,8},{24,16},{32,24},{40,32},{48,40},{56,48},{64,56},{72,6... | collective-permute-start | bytes 61448 | tf_op jit(solution)/shard_map/ppermute | solution.py:20
  18.4 10.4 %copy-start.7 = (s32[4,1024]{1,0:T(4,128)S(1)}, s32[4,1024]{1,0:T(4,128)}, u32[]{:S(2)}) copy-start(s32[4,1024]{1,0:T(4,128)} %param.15) | copy-start | bytes 49156
  18.4 11.1 %copy-start.4 = (f32[20,2,4,128]{3,2,1,0:T(4,128)S(1)}, f32[20,2,4,128]{3,2,1,0:T(4,128)}, u32[]{:S(2)}) copy-start(f32[20,2,4,128]{3,2,1,0:T(4,128)} %param.10) | copy-start | bytes 245764
  18.4 11.1 %collective-permute-start = (f32[20,2,1,128]{3,2,1,0:T(1,128)S(1)}, f32[20,2,1,128]{3,2,1,0:T(1,128)S(1)}, u32[]{:S(2)}, u32[]{:S(2)}) collective-permute-start(f32[20,2,1,128]{3,2,1,0:T(1,128)S(1)} %get-tuple-element.28), channel_id=1, source_target_pairs={{0,8},{8,16},{16,24},{24,32},{32,40},{40,48},{48,56},{56,64},{64,7... | collective-permute-start | bytes 61448 | tf_op jit(solution)/shard_map/ppermute | solution.py:17
  28.8 0.7 copy-start.10
  29.7 4.4 collective-permute-start.3
  31.7 3.4 collective-permute-start.2
  35.5 8.0 copy-start.8
  35.5 8.0 collective-permute-start.5
  41.6 7.8 collective-permute-start.4
  49.4 4.5 copy-start.9
  49.5 4.4 collective-permute-start.7
  51.5 3.4 collective-permute-start.6
  72.5 401.2 %all-reduce.7.cloned.1.call-start = ((), (), s32[]{:S(2)}) async-start(), calls=%async_computation.1 | async-start | bytes 1048576 | tf_op jit(solution)/shard_map/psum | solution.py:75
  263.5 1.3 copy-start
  264.8 0.7 copy-start.5
  264.8 0.7 copy-start.6
  285.1 398.6 %all-reduce.9.cloned.1.call-start = ((), (), s32[]{:S(2)}) async-start(), calls=%async_computation.2 | async-start | bytes 1048576 | tf_op jit(solution)/shard_map/psum | solution.py:75
  473.7 1.3 copy-start.1
  495.0 398.6 %all-reduce.11.cloned.1.call-start = ((), (), s32[]{:S(2)}) async-start(), calls=%async_computation.3 | async-start | bytes 1048576 | tf_op jit(solution)/shard_map/psum | solution.py:75
  683.7 1.3 copy-start.2
  893.6 1.3 copy-start.3
Sparse Core Ops, SparseCore 0:
  72.6 190.7 all-reduce.4
  285.2 188.4 all-reduce.6
  495.2 188.4 all-reduce.8
  705.1 188.4 all-reduce.10
where the time goes:
time: 906 us; the launch traced here: 905 us
  waiting for transfers between devices  764 us (84%)
  blocking collectives  51.8 us (6%)
  starting transfers between devices  29.8 us (3%)
  between operations  21.4 us (2%)
  local copies, waits for them, and re-layouts  15.9 us (2%)
  other arithmetic  12.7 us (1%)
    psum x4, waiting for transfers between devices, local(): prior_obs = lax.psum(jnp.where(is_held[None], picked, 0.0), ('gx', 'gy'))  756 us
    all_gather x4, blocking collectives, local(): gathered = lax.all_gather(stacked, 'ma', axis=0, tiled=True)  51.8 us
    ppermute x4, starting transfers between devices, extended(): lax.ppermute(lax.slice_in_dim(block, 0, width, axis=dim), axis, backward)  20.7 us
  transfers between devices with their start and end apart: 12, of which 7 were waited for; matrix products, arithmetic and copies ran while one was open for 0% of the time, Pallas kernels for 0%

commit v1 on v0

--- a/solution.py
+++ b/solution.py
@@ -72,7 +72,7 @@
         gathered = lax.all_gather(stacked, "ma", axis=0, tiled=True)
         picked = jnp.take(gathered, obs_cell[block_id], axis=1)
         is_held = obs_region[block_id] == own_region
-        prior_obs = lax.psum(jnp.where(is_held[None], picked, 0.0), ("gx", "gy"))
+        prior_obs = lax.psum(lax.psum(jnp.where(is_held[None], picked, 0.0), "gx"), "gy")
         mixing = mixing_matrix(
             prior_obs,
             obs_value[block_id],

time: 906 us -> 915 us (level)
  the two profiles are of different devices: /device:TPU:24 before, /device:TPU:1 now
where the time goes in v1:
time: 915 us; the launch traced here: 914 us
  waiting for transfers between devices  779 us (85%)
  blocking collectives  39.4 us (4%)
  starting transfers between devices  35.9 us (4%)
  between operations  21.8 us (2%)
  local copies, waits for them, and re-layouts  15.9 us (2%)
  other arithmetic  12.7 us (1%)
    psum x4, waiting for transfers between devices, local(): lax.psum(jnp.where(is_held[None], picked, 0.0), 'gx')  611 us
    psum x4, waiting for transfers between devices, local(): lax.psum(lax.psum(jnp.where(is_held[None], picked, 0.0), 'gx'), 'gy')  160 us
    all_gather x4, blocking collectives, local(): gathered = lax.all_gather(stacked, 'ma', axis=0, tiled=True)  39.4 us
    ppermute x4, starting transfers between devices, extended(): lax.ppermute(lax.slice_in_dim(block, 0, width, axis=dim), axis, backward)  27.7 us
  transfers between devices with their start and end apart: 16, of which 11 were waited for; matrix products, arithmetic and copies ran while one was open for 0% of the time, Pallas kernels for 0%

profile of v1, /device:TPU:1, one launch (start us, length us, event | category | flops | bytes accessed | tf_op | source)
XLA Modules:
  0.0 914.2 jit_solution(16888553405415975835)
XLA Ops:
  7.6 14.4 %collective-permute-start.1 = (f32[20,2,1,128]{3,2,1,0:T(1,128)S(1)}, f32[20,2,1,128]{3,2,1,0:T(1,128)S(1)}, u32[]{:S(2)}, u32[]{:S(2)}) collective-permute-start(f32[20,2,1,128]{3,2,1,0:T(1,128)S(1)} %get-tuple-element.29), channel_id=1, source_target_pairs={{8,0},{16,8},{24,16},{32,24},{40,32},{48,40},{56,48},{64,56},{72,6... | collective-permute-start | bytes 61448 | tf_op jit(solution)/shard_map/ppermute | solution.py:20
  22.0 1.9 collective-permute-start
  32.5 2.9 collective-permute-start.3
  35.4 1.9 collective-permute-start.2
  37.4 1.3 collective-permute-done.2
  39.1 7.0 collective-permute-start.5
  46.1 1.9 collective-permute-start.4
  48.1 5.9 collective-permute-done.4
  54.1 3.5 collective-permute-start.7
  57.6 1.9 collective-permute-start.6
  61.3 10.5 %all-gather = f32[4,20,1024]{2,1,0:T(8,128)S(1)} all-gather(f32[1,20,1024]{2,1,0:T(8,128)S(1)} %reshape.117), channel_id=1, replica_groups=mesh['gx'=64,'gy'=2,'ma'=4] {'ma'}, dimensions={0}, use_global_device_ids=true | all-gather | bytes 409600 | tf_op jit(solution)/shard_map/all_gather | solution.py:72
  72.1 2.8 gather_fusion
  76.2 146.6 %all-reduce.9.cloned.1.call-done = f32[80,1024]{0,1:T(8,128)} async-done(((f32[80,1024]{0,1:T(8,128)}), f32[80,1024]{0,1:T(8,128)}) %all-reduce.9.cloned.1.call-update) | async-done | bytes 327696 | tf_op jit(solution)/shard_map/psum | solution.py:75
  223.6 39.6 %all-reduce.11.cloned.1.call-done = f32[80,1024]{0,1:T(8,128)} async-done(((f32[80,1024]{0,1:T(8,128)}), f32[80,1024]{0,1:T(8,128)}) %all-reduce.11.cloned.1.call-update) | async-done | bytes 327696 | tf_op jit(solution)/shard_map/psum | solution.py:75
  263.1 1.3 reduce_sum.108
  265.3 1.5 fusion.6
  267.5 9.6 %all-gather.1 = f32[4,20,1024]{2,1,0:T(8,128)S(1)} all-gather(f32[1,20,1024]{2,1,0:T(8,128)S(1)} %bitcast.71), channel_id=1, replica_groups=mesh['gx'=64,'gy'=2,'ma'=4] {'ma'}, dimensions={0}, use_global_device_ids=true | all-gather | bytes 409600 | tf_op jit(solution)/shard_map/all_gather | solution.py:72
  277.4 2.8 gather_fusion.1
  281.5 154.7 %all-reduce.13.cloned.1.call-done = f32[80,1024]{0,1:T(8,128)} async-done(((f32[80,1024]{0,1:T(8,128)}), f32[80,1024]{0,1:T(8,128)}) %all-reduce.13.cloned.1.call-update) | async-done | bytes 327696 | tf_op jit(solution)/shard_map/psum | solution.py:75
  436.4 40.1 %all-reduce.15.cloned.1.call-done = f32[80,1024]{0,1:T(8,128)} async-done(((f32[80,1024]{0,1:T(8,128)}), f32[80,1024]{0,1:T(8,128)}) %all-reduce.15.cloned.1.call-update) | async-done | bytes 327696 | tf_op jit(solution)/shard_map/psum | solution.py:75
  476.5 1.3 reduce_sum.111
  478.3 1.5 fusion.4
  480.5 9.6 %all-gather.2 = f32[4,20,1024]{2,1,0:T(8,128)S(1)} all-gather(f32[1,20,1024]{2,1,0:T(8,128)S(1)} %bitcast.73), channel_id=1, replica_groups=mesh['gx'=64,'gy'=2,'ma'=4] {'ma'}, dimensions={0}, use_global_device_ids=true | all-gather | bytes 409600 | tf_op jit(solution)/shard_map/all_gather | solution.py:72
  490.4 2.8 gather_fusion.2
  494.5 154.8 %all-reduce.17.cloned.1.call-done = f32[80,1024]{0,1:T(8,128)} async-done(((f32[80,1024]{0,1:T(8,128)}), f32[80,1024]{0,1:T(8,128)}) %all-reduce.17.cloned.1.call-update) | async-done | bytes 327696 | tf_op jit(solution)/shard_map/psum | solution.py:75
  649.5 39.9 %all-reduce.19.cloned.1.call-done = f32[80,1024]{0,1:T(8,128)} async-done(((f32[80,1024]{0,1:T(8,128)}), f32[80,1024]{0,1:T(8,128)}) %all-reduce.19.cloned.1.call-update) | async-done | bytes 327696 | tf_op jit(solution)/shard_map/psum | solution.py:75
  691.3 1.5 fusion.2
  693.5 9.6 %all-gather.3 = f32[4,20,1024]{2,1,0:T(8,128)S(1)} all-gather(f32[1,20,1024]{2,1,0:T(8,128)S(1)} %bitcast.72), channel_id=1, replica_groups=mesh['gx'=64,'gy'=2,'ma'=4] {'ma'}, dimensions={0}, use_global_device_ids=true | all-gather | bytes 409600 | tf_op jit(solution)/shard_map/all_gather | solution.py:72
  703.4 2.8 gather_fusion.3
  707.5 154.8 %all-reduce.21.cloned.1.call-done = f32[80,1024]{0,1:T(8,128)} async-done(((f32[80,1024]{0,1:T(8,128)}), f32[80,1024]{0,1:T(8,128)}) %all-reduce.21.cloned.1.call-update) | async-done | bytes 327696 | tf_op jit(solution)/shard_map/psum | solution.py:75
  862.3 40.3 %all-reduce.23.cloned.1.call-done = f32[80,1024]{0,1:T(8,128)} async-done(((f32[80,1024]{0,1:T(8,128)}), f32[80,1024]{0,1:T(8,128)}) %all-reduce.23.cloned.1.call-update) | async-done | bytes 327696 | tf_op jit(solution)/shard_map/psum | solution.py:75
  904.4 1.5 fusion
  (118 shorter events, 19.8 us)
Async XLA Ops:
  6.5 25.8 %copy-start.4 = (f32[20,2,4,128]{3,2,1,0:T(4,128)S(1)}, f32[20,2,4,128]{3,2,1,0:T(4,128)}, u32[]{:S(2)}) copy-start(f32[20,2,4,128]{3,2,1,0:T(4,128)} %param.10) | copy-start | bytes 245764
  6.5 216.2 %all-reduce.9.cloned.1.call-start = ((), (), s32[]{:S(2)}) async-start(), calls=%async_computation | async-start | bytes 1048576 | tf_op jit(solution)/shard_map/psum | solution.py:75
  7.6 16.4 %copy-start.11 = (s32[4]{0:T(128)S(1)}, s32[4]{0:T(128)}, u32[]{:S(2)}) copy-start(s32[4]{0:T(128)} %param.16) | copy-start | bytes 52
  7.6 24.7 %collective-permute-start.1 = (f32[20,2,1,128]{3,2,1,0:T(1,128)S(1)}, f32[20,2,1,128]{3,2,1,0:T(1,128)S(1)}, u32[]{:S(2)}, u32[]{:S(2)}) collective-permute-start(f32[20,2,1,128]{3,2,1,0:T(1,128)S(1)} %get-tuple-element.29), channel_id=1, source_target_pairs={{8,0},{16,8},{24,16},{32,24},{40,32},{48,40},{56,48},{64,56},{72,6... | collective-permute-start | bytes 61448 | tf_op jit(solution)/shard_map/ppermute | solution.py:20
  22.0 10.3 %collective-permute-start = (f32[20,2,1,128]{3,2,1,0:T(1,128)S(1)}, f32[20,2,1,128]{3,2,1,0:T(1,128)S(1)}, u32[]{:S(2)}, u32[]{:S(2)}) collective-permute-start(f32[20,2,1,128]{3,2,1,0:T(1,128)S(1)} %get-tuple-element.28), channel_id=1, source_target_pairs={{0,8},{8,16},{16,24},{24,32},{32,40},{40,48},{48,56},{56,64},{64,7... | collective-permute-start | bytes 61448 | tf_op jit(solution)/shard_map/ppermute | solution.py:17
  27.3 2.4 copy-start.10
  29.7 2.6 copy-start.7
  32.5 4.8 collective-permute-start.3
  35.4 3.3 collective-permute-start.2
  39.1 8.9 collective-permute-start.5
  46.1 7.8 collective-permute-start.4
  54.0 5.6 copy-start.8
  54.1 5.5 collective-permute-start.7
  57.6 3.3 collective-permute-start.6
  76.1 187.0 %all-reduce.11.cloned.1.call-start = ((), (), s32[]{:S(2)}) async-start(), calls=%async_computation.1 | async-start | bytes 1048576 | tf_op jit(solution)/shard_map/psum | solution.py:75
  222.7 0.7 copy-start.9
  222.7 213.5 %all-reduce.13.cloned.1.call-start = ((), (), s32[]{:S(2)}) async-start(), calls=%async_computation.2 | async-start | bytes 1048576 | tf_op jit(solution)/shard_map/psum | solution.py:75
  263.1 1.3 copy-start
  264.5 0.7 copy-start.5
  264.5 0.7 copy-start.6
  281.4 195.1 %all-reduce.15.cloned.1.call-start = ((), (), s32[]{:S(2)}) async-start(), calls=%async_computation.3 | async-start | bytes 1048576 | tf_op jit(solution)/shard_map/psum | solution.py:75
  436.2 213.0 %all-reduce.17.cloned.1.call-start = ((), (), s32[]{:S(2)}) async-start(), calls=%async_computation.4 | async-start | bytes 1048576 | tf_op jit(solution)/shard_map/psum | solution.py:75
  476.5 1.3 copy-start.1
  494.4 195.1 %all-reduce.19.cloned.1.call-start = ((), (), s32[]{:S(2)}) async-start(), calls=%async_computation.5 | async-start | bytes 1048576 | tf_op jit(solution)/shard_map/psum | solution.py:75
  649.2 213.0 %all-reduce.21.cloned.1.call-start = ((), (), s32[]{:S(2)}) async-start(), calls=%async_computation.6 | async-start | bytes 1048576 | tf_op jit(solution)/shard_map/psum | solution.py:75
  689.5 1.3 copy-start.2
  707.4 195.2 %all-reduce.23.cloned.1.call-start = ((), (), s32[]{:S(2)}) async-start(), calls=%async_computation.7 | async-start | bytes 1048576 | tf_op jit(solution)/shard_map/psum | solution.py:75
  902.6 1.3 copy-start.3
Sparse Core Ops, SparseCore 0:
  76.2 146.4 all-reduce.8
  225.9 37.2 all-reduce.10
  281.5 154.6 all-reduce.12
  439.2 37.2 all-reduce.14
  494.5 154.6 all-reduce.16
  652.2 37.2 all-reduce.18
  707.5 154.6 all-reduce.20
  865.4 37.2 all-reduce.22
